TPU v7x, 512 devices: a whole 4x8x8 slice. The times are simulated.
512 devices in a mesh: head: 4 (over x), blk: 128 (over y, z, core).
Axes of the slice: x: 4, y: 8, z: 8, core: 2. Of those that a mesh axis runs over, the one named last changes fastest.
Arguments:
- tokens: bfloat16 [8192, 2048], P('blk'), may hold values from -6 to 6
- q_weight: bfloat16 [2048, 1024], P(None, 'head')
- k_weight: bfloat16 [2048, 256], P(None, 'head')
- v_weight: bfloat16 [2048, 256], P(None, 'head'), may hold values from -0.125 to 0.125
- o_weight: bfloat16 [1024, 2048], P('head'), may hold values from -0.1875 to 0.1875
- kv_pages: bfloat16 [4, 384, 64, 128], P('head', 'blk')
- page_node: int32 [384], replicated, may hold values from 0 to 72, as said below
- page_fill: int32 [384], replicated, may hold values from 1 to 64
- req_len: int32 [64], replicated, may hold values from 1 to 256, 8192 in all
- req_leaf: int32 [64], replicated, may hold values from 0 to 63
- leaf_parent: int32 [64], replicated, may hold values from 0 to 7
Outputs:
- attn_out: bfloat16 [8192, 2048], P('blk', 'head')
Inputs may be any that keep to these rules, and one draw needn't show every extreme that they name: `req_len`: their sum is 8192, and the longest request has exactly 256 tokens. `page_node`: node 0 is the root, nodes 1 to 8 form the middle level and the rest are leaves; the root holds a third of the 384 pages, each middle node a 1 / 8 share of another third, each leaf two pages, placed over the pages in any order.
All inputs are finite; a program needn't handle non-finite values.
Results may differ from a plain program's by a relative error of at most 0.012.
The roundings to bfloat16 on the way count: a program that leaves them out, or rounds other values in their place, can miss the bound.
Values may be sent and summed in bfloat16 or wider, within the bound.
A program may use at most 128 MiB of HBM per device.

v0:
```python
import jax
import jax.numpy as jnp
from jax import lax
from jax.sharding import PartitionSpec as P

HD = 64
MIDS = 8
PROMPT = 256


NEGATIVE = -1e30
EPSILON = 1e-06
ROPE_BASE = 10000.0
SCORE_SCALE = 0.125


def shifted(value, axis, steps):
    count = lax.axis_size(axis)
    first, last = (max(0, -steps), min(count, count - steps))
    return lax.ppermute(value, axis, [(source, source + steps) for source in range(first, last)])


def norm_rows(hidden):
    wide = hidden.astype(jnp.float32)
    return (wide * lax.rsqrt(jnp.mean(wide * wide, axis=-1, keepdims=True) + EPSILON)).astype(
        jnp.bfloat16
    )


def rotate(values, positions):
    half_dim = values.shape[-1] // 2
    frequency = ROPE_BASE ** (-jnp.arange(half_dim).astype(jnp.float32) / half_dim)
    angles = positions.astype(jnp.float32)[:, None] * frequency[None, :]
    cosine = jnp.cos(angles)[:, None, :]
    sine_part = jnp.sin(angles)[:, None, :]
    first_half = values[..., :half_dim]
    second = values[..., half_dim:]
    return jnp.concatenate(
        [first_half * cosine - second * sine_part, second * cosine + first_half * sine_part],
        axis=-1,
    )


def request_of(places, req_len):
    req_end = jnp.cumsum(req_len)
    return jnp.sum((places[:, None] >= req_end[None, :]).astype(jnp.int32), axis=1)


def row_paths(places, req_len, req_leaf, leaf_parent, page_node, page_fill):
    req_count = req_len.shape[0]
    leaf_count = leaf_parent.shape[0]
    node_count = 1 + MIDS + leaf_count
    starts = jnp.cumsum(req_len) - req_len
    request = request_of(places, req_len)
    chosen = request[:, None] == jnp.arange(req_count, dtype=jnp.int32)[None, :]
    offset = places - jnp.sum(jnp.where(chosen, starts[None, :], 0), axis=1)
    leaf_id = jnp.sum(jnp.where(chosen, req_leaf[None, :], 0), axis=1)
    leaf_hit = leaf_id[:, None] == jnp.arange(leaf_count, dtype=jnp.int32)[None, :]
    mid_id = jnp.sum(jnp.where(leaf_hit, leaf_parent[None, :], 0), axis=1)
    path_ids = jnp.stack([jnp.zeros_like(mid_id), 1 + mid_id, 1 + MIDS + leaf_id], axis=1)
    node_hit = page_node[:, None] == jnp.arange(node_count, dtype=jnp.int32)[None, :]
    node_len = jnp.sum(jnp.where(node_hit, page_fill[:, None], 0), axis=0)
    on_path = path_ids[:, :, None] == jnp.arange(node_count, dtype=jnp.int32)[None, None, :]
    prefix = jnp.sum(jnp.where(on_path, node_len[None, None, :], 0), axis=(1, 2))
    return (request, path_ids, prefix + offset)


def page_mask(path_ids, nodes_here, fills_here, page_len):
    node_hit = jnp.any(path_ids[:, :, None] == nodes_here[None, None, :], axis=1)
    slot_live = jnp.arange(page_len, dtype=jnp.int32)[None, :] < fills_here[:, None]
    return (node_hit[:, :, None] & slot_live[None, :, :]).reshape(path_ids.shape[0], -1)


def block_size(total_pages, page_limit):
    chosen = 1
    for trial_size in range(1, min(total_pages, page_limit) + 1):
        if total_pages % trial_size == 0:
            chosen = trial_size
    return chosen


def fold_keys(running, q_rot, key_rows, values, allowed):
    top_old, total_old, accum_old = running
    scores = (
        jnp.einsum("rkhd,knd->khrn", q_rot, key_rows, preferred_element_type=jnp.float32)
        * SCORE_SCALE
    )
    scores = jnp.where(allowed[None, None], scores, NEGATIVE)
    top_new = jnp.maximum(top_old, jnp.max(scores, axis=-1))
    weights = jnp.where(allowed[None, None], jnp.exp(scores - top_new[..., None]), 0.0)
    factor = jnp.exp(top_old - top_new)
    total_new = total_old * factor + jnp.sum(weights, axis=-1)
    product = jnp.einsum(
        "khrn,knd->khrd", weights.astype(jnp.bfloat16), values, preferred_element_type=jnp.float32
    )
    return (top_new, total_new, accum_old * factor[..., None] + product)


def local(
    tokens,
    q_weight,
    k_weight,
    v_weight,
    o_weight,
    kv_pages,
    page_node,
    page_fill,
    req_len,
    req_leaf,
    leaf_parent,
):
    local_rows = tokens.shape[0]
    kv_heads = k_weight.shape[1] // HD
    q_heads = q_weight.shape[1] // HD
    group_size = q_heads // kv_heads
    page_len = kv_pages.shape[2]
    blk_index = lax.axis_index("blk")
    places = blk_index * local_rows + jnp.arange(local_rows, dtype=jnp.int32)
    request, path_ids, positions = row_paths(
        places, req_len, req_leaf, leaf_parent, page_node, page_fill
    )
    normed = norm_rows(tokens)
    queries = jnp.dot(normed, q_weight, preferred_element_type=jnp.float32).reshape(
        local_rows, q_heads, HD
    )
    q_rot = (
        rotate(queries, positions)
        .astype(jnp.bfloat16)
        .reshape(local_rows, kv_heads, group_size, HD)
    )
    keys_new = jnp.dot(normed, k_weight, preferred_element_type=jnp.float32).reshape(
        local_rows, kv_heads, HD
    )
    keys_new = rotate(keys_new, positions).astype(jnp.bfloat16)
    values_new = (
        jnp.dot(normed, v_weight, preferred_element_type=jnp.float32)
        .astype(jnp.bfloat16)
        .reshape(local_rows, kv_heads, HD)
    )
    own_pack = jnp.concatenate([keys_new, values_new], axis=-1)
    reach_devs = (PROMPT - 1) // local_rows + 1
    near_packs = [own_pack]
    near_places = [places]
    for distance in range(1, reach_devs + 1):
        near_packs.insert(0, shifted(own_pack, "blk", distance))
        near_places.insert(0, places - distance * local_rows)
    near_pack = jnp.swapaxes(jnp.concatenate(near_packs, axis=0), 0, 1)
    near_place = jnp.concatenate(near_places)
    near_req = request_of(jnp.maximum(near_place, 0), req_len)
    near_ok = (
        (near_place[None, :] >= 0)
        & (near_req[None, :] == request[:, None])
        & (near_place[None, :] <= places[:, None])
    )
    start_state = (
        jnp.full((kv_heads, group_size, local_rows), NEGATIVE, jnp.float32),
        jnp.zeros((kv_heads, group_size, local_rows), jnp.float32),
        jnp.zeros((kv_heads, group_size, local_rows, HD), jnp.float32),
    )
    running = fold_keys(start_state, q_rot, near_pack[..., :HD], near_pack[..., HD:], near_ok)
    group_limit = max(1, 2048 // page_len)
    shard_pages = lax.all_gather(kv_pages, "blk", axis=1, tiled=True)
    page_total = shard_pages.shape[1]
    group_pages = block_size(page_total, group_limit)

    def one_group(group_index, inner):
        first_page = group_index * group_pages
        page_block = lax.dynamic_slice_in_dim(shard_pages, first_page, group_pages, 1)
        nodes_here = lax.dynamic_slice_in_dim(page_node, first_page, group_pages, 0)
        fills_here = lax.dynamic_slice_in_dim(page_fill, first_page, group_pages, 0)
        allowed = page_mask(path_ids, nodes_here, fills_here, page_len)
        flat_block = page_block.reshape(kv_heads, group_pages * page_len, 2 * HD)
        return fold_keys(inner, q_rot, flat_block[..., :HD], flat_block[..., HD:], allowed)

    running = lax.fori_loop(0, page_total // group_pages, one_group, running)
    top_all, total_all, accum_all = running
    attended = accum_all / total_all[..., None]
    attended = (
        jnp.transpose(attended, (2, 0, 1, 3)).reshape(local_rows, q_heads * HD).astype(jnp.bfloat16)
    )
    partial_out = jnp.dot(attended, o_weight, preferred_element_type=jnp.float32)
    return lax.psum_scatter(partial_out, "head", scatter_dimension=1, tiled=True).astype(
        jnp.bfloat16
    )


def solution(mesh):
    return jax.shard_map(
        local,
        mesh=mesh,
        in_specs=(
            P("blk", None),
            P(None, "head"),
            P(None, "head"),
            P(None, "head"),
            P("head", None),
            P("head", "blk", None, None),
            P(),
            P(),
            P(),
            P(),
            P(),
        ),
        out_specs=P("blk", "head"),
        check_vma=False,
    )
```

profile of v0, /device:TPU:1, one launch (start us, length us, event | category | flops | bytes accessed | tf_op | source)
XLA Modules:
  0.0 204.6 jit_solution(11109464322911127699)
XLA Ops:
  9.1 0.8 select_reduce_fusion.2
  10.0 0.8 select_reduce_fusion.3
  10.8 0.8 select_reduce_fusion
  11.9 1.1 fusion.17
  13.1 1.3 convolution_bitcast_fusion.1
  14.8 1.3 fusion.16
  16.2 5.4 %collective-permute-start.3 = (bf16[64,1,128]{2,0,1:T(8,128)(2,1)S(1)}, bf16[64,1,128]{2,0,1:T(8,128)(2,1)S(1)}, u32[]{:S(2)}, u32[]{:S(2)}) collective-permute-start(bf16[64,1,128]{2,0,1:T(8,128)(2,1)S(1)} %pad_maximum_fusion.1), channel_id=1, source_target_pairs={{0,1},{1,2},{2,3},{3,4},{4,5},{5,6},{6,7},{7,8},{8,9},{9,10},{10,1... | collective-permute-start | bytes 49160 | tf_op jit(solution)/shard_map/ppermute | solution.py:20
  21.6 4.0 %collective-permute-start.2 = (bf16[64,1,128]{2,0,1:T(8,128)(2,1)S(1)}, bf16[64,1,128]{2,0,1:T(8,128)(2,1)S(1)}, u32[]{:S(2)}, u32[]{:S(2)}) collective-permute-start(bf16[64,1,128]{2,0,1:T(8,128)(2,1)S(1)} %pad_maximum_fusion.1), channel_id=1, source_target_pairs={{0,2},{1,3},{2,4},{3,5},{4,6},{5,7},{6,8},{7,9},{8,10},{9,11},{10,... | collective-permute-start | bytes 49160 | tf_op jit(solution)/shard_map/ppermute | solution.py:20
  25.6 4.0 %collective-permute-start.1 = (bf16[64,1,128]{2,0,1:T(8,128)(2,1)S(1)}, bf16[64,1,128]{2,0,1:T(8,128)(2,1)S(1)}, u32[]{:S(2)}, u32[]{:S(2)}) collective-permute-start(bf16[64,1,128]{2,0,1:T(8,128)(2,1)S(1)} %pad_maximum_fusion.1), channel_id=1, source_target_pairs={{0,3},{1,4},{2,5},{3,6},{4,7},{5,8},{6,9},{7,10},{8,11},{9,12},{10... | collective-permute-start | bytes 49160 | tf_op jit(solution)/shard_map/ppermute | solution.py:20
  29.6 6.1 %collective-permute-start = (bf16[64,1,128]{2,0,1:T(8,128)(2,1)S(1)}, bf16[64,1,128]{2,0,1:T(8,128)(2,1)S(1)}, u32[]{:S(2)}, u32[]{:S(2)}) collective-permute-start(bf16[64,1,128]{2,0,1:T(8,128)(2,1)S(1)} %pad_maximum_fusion.1), channel_id=1, source_target_pairs={{0,4},{1,5},{2,6},{3,7},{4,8},{5,9},{6,10},{7,11},{8,12},{9,13},{1... | collective-permute-start | bytes 49160 | tf_op jit(solution)/shard_map/ppermute | solution.py:20
  35.7 1.7 fusion.41
  39.3 63.6 %all-gather.2.cloned.1.call-done = bf16[1,384,64,128]{3,2,0,1:T(8,128)(2,1)} async-done(((bf16[1,3,64,128]{3,2,0,1:T(8,128)(2,1)}), bf16[1,384,64,128]{3,2,0,1:T(8,128)(2,1)}) %all-gather.2.cloned.1.call-update) | async-done | bytes 6291472 | tf_op jit(solution)/shard_map/all_gather | solution.py:162
  103.0 70.1 %while.17 = (s32[]{:T(128)}, f32[1,4,64]{2,1,0:T(4,128)S(1)}, f32[1,4,64]{2,1,0:T(4,128)S(1)}, f32[1,4,64,64]{3,2,1,0:T(8,128)S(1)}, s32[64,3]{0,1:T(4,128)S(1)}...) while((s32[]{:T(128)}, f32[1,4,64]{2,1,0:T(4,128)S(1)}, ...), condition=%wide.region_15.16_spmd, body=%wide.region_11.15_spmd.sunk | while | flops 139113216 | bytes 9696951 | solution.py:175
  105.8 1.1 constant_dynamic-slice_fusion.2
  108.8 0.8 dynamic_slice.27
  111.7 1.1 constant_dynamic-slice_fusion.2
  117.5 1.1 constant_dynamic-slice_fusion.2
  123.4 1.1 constant_dynamic-slice_fusion.2
  129.2 1.1 constant_dynamic-slice_fusion.2
  135.1 1.1 constant_dynamic-slice_fusion.2
  138.0 0.8 dynamic_slice.27
  140.9 1.1 constant_dynamic-slice_fusion.2
  146.8 1.1 constant_dynamic-slice_fusion.2
  149.7 0.8 dynamic_slice.27
  152.6 1.1 constant_dynamic-slice_fusion.2
  158.4 1.1 constant_dynamic-slice_fusion.2
  161.4 0.8 dynamic_slice.27
  164.3 1.1 constant_dynamic-slice_fusion.2
  170.1 1.1 constant_dynamic-slice_fusion.2
  173.4 1.1 fusion.48
  174.5 21.7 %reduce-scatter.2.cloned.1.call-done = f32[64,512]{1,0:T(8,128)} async-done(((f32[64,2048]{1,0:T(8,128)}), f32[64,512]{1,0:T(8,128)}) %reduce-scatter.2.cloned.1.call-update) | async-done | bytes 131088 | tf_op jit(solution)/shard_map/reduce_scatter | solution.py:182
  196.2 1.5 convert_element_type.84
  (265 shorter events, 58.6 us)
Async XLA Ops:
  6.5 166.8 %copy-start = (bf16[256,2048]{1,0:T(8,128)(2,1)S(1)}, bf16[256,2048]{1,0:T(8,128)(2,1)}, u32[]{:S(2)}) copy-start(bf16[256,2048]{1,0:T(8,128)(2,1)} %param.17) | copy-start | bytes 3145732
  6.5 96.4 %all-gather.2.cloned.1.call-start = ((), (), s32[]{:S(2)}) async-start(), calls=%async_computation.1 | async-start | bytes 6340608 | tf_op jit(solution)/shard_map/all_gather | solution.py:162
  7.3 188.9 %reduce-scatter.2.cloned.1.call-start = ((), (), s32[]{:S(2)}) async-start(), calls=%async_computation.2 | async-start | bytes 655360 | tf_op jit(solution)/shard_map/reduce_scatter | solution.py:182
  16.2 22.2 %collective-permute-start.3 = (bf16[64,1,128]{2,0,1:T(8,128)(2,1)S(1)}, bf16[64,1,128]{2,0,1:T(8,128)(2,1)S(1)}, u32[]{:S(2)}, u32[]{:S(2)}) collective-permute-start(bf16[64,1,128]{2,0,1:T(8,128)(2,1)S(1)} %pad_maximum_fusion.1), channel_id=1, source_target_pairs={{0,1},{1,2},{2,3},{3,4},{4,5},{5,6},{6,7},{7,8},{8,9},{9,10},{10,1... | collective-permute-start | bytes 49160 | tf_op jit(solution)/shard_map/ppermute | solution.py:20
  21.6 16.8 %collective-permute-start.2 = (bf16[64,1,128]{2,0,1:T(8,128)(2,1)S(1)}, bf16[64,1,128]{2,0,1:T(8,128)(2,1)S(1)}, u32[]{:S(2)}, u32[]{:S(2)}) collective-permute-start(bf16[64,1,128]{2,0,1:T(8,128)(2,1)S(1)} %pad_maximum_fusion.1), channel_id=1, source_target_pairs={{0,2},{1,3},{2,4},{3,5},{4,6},{5,7},{6,8},{7,9},{8,10},{9,11},{10,... | collective-permute-start | bytes 49160 | tf_op jit(solution)/shard_map/ppermute | solution.py:20
  25.6 12.8 %collective-permute-start.1 = (bf16[64,1,128]{2,0,1:T(8,128)(2,1)S(1)}, bf16[64,1,128]{2,0,1:T(8,128)(2,1)S(1)}, u32[]{:S(2)}, u32[]{:S(2)}) collective-permute-start(bf16[64,1,128]{2,0,1:T(8,128)(2,1)S(1)} %pad_maximum_fusion.1), channel_id=1, source_target_pairs={{0,3},{1,4},{2,5},{3,6},{4,7},{5,8},{6,9},{7,10},{8,11},{9,12},{10... | collective-permute-start | bytes 49160 | tf_op jit(solution)/shard_map/ppermute | solution.py:20
  29.6 8.7 %collective-permute-start = (bf16[64,1,128]{2,0,1:T(8,128)(2,1)S(1)}, bf16[64,1,128]{2,0,1:T(8,128)(2,1)S(1)}, u32[]{:S(2)}, u32[]{:S(2)}) collective-permute-start(bf16[64,1,128]{2,0,1:T(8,128)(2,1)S(1)} %pad_maximum_fusion.1), channel_id=1, source_target_pairs={{0,4},{1,5},{2,6},{3,7},{4,8},{5,9},{6,10},{7,11},{8,12},{9,13},{1... | collective-permute-start | bytes 49160 | tf_op jit(solution)/shard_map/ppermute | solution.py:20
Sparse Core Ops, SparseCore 0:
  10.5 92.4 all-gather.1
  174.6 21.5 reduce-scatter.1
where the time goes:
time: 207 us; the launch traced here: 205 us
  waiting for transfers between devices  86.1 us (42%)
  local copies, waits for them, and re-layouts  47 us (23%)
  matrix products  21.1 us (10%)
  starting transfers between devices  19.6 us (9%)
  other arithmetic  16.3 us (8%)
  between operations  13.7 us (7%)
    all_gather x1, waiting for transfers between devices, local(): shard_pages = lax.all_gather(kv_pages, 'blk', axis=1, tiled=True)  63.6 us
    reduce_scatter x1, waiting for transfers between devices, local(): lax.psum_scatter(partial_out, 'head', scatter_dimension=1, tiled=True)  21.7 us
    ppermute x4, starting transfers between devices, shifted(): lax.ppermute(value, axis, [(source, source + steps) for source in range(f...  19.5 us
    dynamic_slice x12, local copies, waits for them, and re-layouts, one_group(): lax.dynamic_slice_in_dim(shard_pages, first_page, group_pages, 1)  13 us
    and x24, local copies, waits for them, and re-layouts, page_mask(): node_hit[:, :, None] & slot_live[None, :, :]  9.91 us
    dynamic_slice x12, local copies, waits for them, and re-layouts, one_group(): fills_here = lax.dynamic_slice_in_dim(page_fill, first_page, group_pages, 0)  9.1 us
    dynamic_slice x12, local copies, waits for them, and re-layouts, one_group(): nodes_here = lax.dynamic_slice_in_dim(page_node, first_page, group_pages, 0)  9.04 us
    dot_general x13, matrix products, fold_keys(): jnp.einsum('khrn,knd->khrd', weights.astype(jnp.bfloat16), values, prefer...  8.64 us
  transfers between devices with their start and end apart: 6, of which 2 were waited for; matrix products, arithmetic and copies ran while one was open for 6% of the time, Pallas kernels for 0%

commit v1 on v0

v1 whole, which is shorter than its diff:
```python
import functools

import jax
import jax.numpy as jnp
import numpy as np
from jax import lax
from jax.experimental import pallas as pl
from jax.experimental.pallas import tpu as pltpu
from jax.sharding import PartitionSpec as P

HD = 64
MIDS = 8
LANES = 128
LINES = {128: (8, 8), 8: (2, 2)}
NEGATIVE = -1e30
EPSILON = 1e-06
ROPE_BASE = 10000.0
SCORE_SCALE = 0.125
MESH = pl.DeviceIdType.MESH
F32 = jnp.float32
BF16 = jnp.bfloat16
I32 = jnp.int32


def offset_at(place, count):
    if isinstance(place, int):
        half = (place + 1) // 2
        return half if place % 2 else (count - half) % count
    half = lax.div(place + 1, 2)
    odd = lax.rem(place, 2)
    return lax.rem(odd * half + (1 - odd) * (count - half), count)


def mirror(place, count):
    if isinstance(place, int):
        if place in (0, count - 1):
            return place
        return place + 1 if place % 2 else place - 1
    odd = lax.rem(place, 2)
    ends = jnp.logical_or(place == 0, place == count - 1)
    return jnp.where(ends, place, place + 2 * odd - 1)


def iota(shape, axis):
    return lax.broadcasted_iota(I32, shape, axis)


def kernel(
    sizes,
    tok,
    wq,
    wk,
    wv,
    wo,
    pages,
    node_hbm,
    fill_hbm,
    len_hbm,
    leaf_hbm,
    parent_hbm,
    freq_hbm,
    out,
    tok_v,
    wq_v,
    wk_v,
    wv_v,
    node_s,
    fill_s,
    node_v,
    fill_v,
    len_v,
    leaf_v,
    parent_v,
    freq_v,
    kvb,
    keys,
    vals,
    near,
    qbuf,
    hot,
    qaug,
    state_top,
    state_sum,
    part,
    part_lse,
    got,
    got_lse,
    own_part,
    att,
    wob,
    loc,
    kv_ss,
    kv_rs,
    fw_ss,
    fw_rs,
    q_ss,
    q_rs,
    nr_ss,
    nr_rs,
    o_ss,
    o_rs,
    l_ss,
    l_rs,
    w_ss,
    w_rs,
    a_ss,
    a_rs,
):
    nx, ny, nz, rows, heads = sizes
    group = heads * rows
    out_cols = out.shape[1]
    n_blk = ny * nz * 2
    hx = lax.axis_index("head")
    blk = lax.axis_index("blk")
    core = lax.rem(blk, 2)
    zi = lax.rem(lax.div(blk, 2), nz)
    yi = lax.div(blk, 2 * nz)

    def blk_of(y, z, c):
        return (y * nz + z) * 2 + c

    def y_peer(place):
        return blk_of(lax.rem(yi + offset_at(place, ny), ny), zi, core)

    def z_peer(place):
        return blk_of(yi, lax.rem(zi + offset_at(place, nz), nz), core)

    sibling = blk_of(yi, zi, 1 - core)

    barrier = pltpu.get_barrier_semaphore()
    greeted = [sibling]
    greeted += [y_peer(place) for place in range(1, ny)]
    greeted += [z_peer(place) for place in range(1, nz)]
    for step in range(1, 5):
        if step < n_blk:
            greeted += [lax.rem(blk + step, n_blk), lax.rem(blk + n_blk - step, n_blk)]
    for peer in greeted:
        pl.semaphore_signal(barrier, inc=1, device_id=(hx, peer), device_id_type=MESH)
    for step in range(1, nx):
        pl.semaphore_signal(
            barrier, inc=1, device_id=(lax.rem(hx + step, nx), blk), device_id_type=MESH
        )

    copies = [
        pltpu.make_async_copy(src, dst, loc.at[at])
        for at, (src, dst) in enumerate(
            [
                (len_hbm, len_v),
                (leaf_hbm, leaf_v),
                (parent_hbm, parent_v),
                (node_hbm, node_v),
                (fill_hbm, fill_v),
                (freq_hbm, freq_v),
                (node_hbm.at[0], node_s),
                (fill_hbm.at[0], fill_s),
                (tok, tok_v),
                (wq, wq_v),
                (wk, wk_v),
                (wv, wv_v),
                (pages.at[0], kvb.at[0]),
                (wo.at[:, pl.ds(pl.multiple_of(hx * out_cols, LANES), out_cols)], wob.at[hx]),
            ]
        )
    ]
    for copy in copies:
        copy.start()

    def remote(src, dst, send, recv, to_head, to_blk):
        return pltpu.make_async_remote_copy(
            src_ref=src,
            dst_ref=dst,
            send_sem=send,
            recv_sem=recv,
            device_id=(to_head, to_blk),
            device_id_type=MESH,
        )

    def kv_copy(place):
        back = mirror(place, ny)
        return remote(
            pages.at[0], kvb.at[2 * back], kv_ss.at[place], kv_rs.at[back], hx, y_peer(place)
        )

    def forward(place):
        src = pages.at[0] if isinstance(place, int) and place == 0 else kvb.at[2 * place]
        return remote(src, kvb.at[2 * place + 1], fw_ss.at[place], fw_rs.at[place], hx, sibling)

    def wo_copy(step):
        to = lax.rem(hx + step, nx)
        cols = pl.ds(pl.multiple_of(to * out_cols, LANES), out_cols)
        return remote(wo.at[:, cols], wob.at[hx], w_ss.at[step], w_rs.at[step], to, blk)

    def near_copy(step):
        to = lax.rem(blk + step, n_blk)
        return remote(near.at[4], near.at[4 - step], nr_ss.at[step], nr_rs.at[step], hx, to)

    def q_copy(place):
        back = mirror(place, nz)
        return remote(
            qbuf.at[0], qbuf.at[back], q_ss.at[place], q_rs.at[back], hx, z_peer(place)
        )

    def part_copies(place):
        back = mirror(place, nz)
        to = z_peer(place)
        return (
            remote(part.at[place], got.at[back], o_ss.at[place], o_rs.at[back], hx, to),
            remote(part_lse.at[place], got_lse.at[back], l_ss.at[place], l_rs.at[back], hx, to),
        )

    def att_copy(step):
        to = lax.rem(hx + step, nx)
        return remote(att.at[hx], att.at[hx], a_ss.at[step], a_rs.at[step], to, blk)

    pl.semaphore_wait(barrier, len(greeted) + nx - 1)
    for place in range(1, ny):
        kv_copy(place).start()
    forward(0).start()
    for step in range(1, nx):
        wo_copy(step).start()

    for copy in copies[:6]:
        copy.wait()
    reqs = len_v.shape[1]
    leaves = parent_v.shape[1]
    diag = iota((reqs, reqs), 0) == iota((reqs, reqs), 1)

    def to_column(row):
        return jnp.sum(jnp.where(diag, row, 0), axis=1, keepdims=True)

    def to_row(column):
        return jnp.sum(jnp.where(diag, column, 0), axis=0, keepdims=True)

    len_row = len_v[...]
    len_col = to_column(len_row)
    upto = iota((reqs, reqs), 0) <= iota((reqs, reqs), 1)
    end_row = jnp.sum(jnp.where(upto, len_col, 0), axis=0, keepdims=True)
    start_row = end_row - len_row
    leaf_col = to_column(leaf_v[...])
    leaf_hit = leaf_col == iota((reqs, leaves), 1)
    mid_col = jnp.sum(jnp.where(leaf_hit, parent_v[...], 0), axis=1, keepdims=True)
    node_row = node_v[...]
    on_path = (node_row == 0) | (node_row == 1 + mid_col) | (node_row == 1 + MIDS + leaf_col)
    prefix_col = jnp.sum(jnp.where(on_path, fill_v[...], 0), axis=1, keepdims=True)
    shift_row = to_row(prefix_col) - start_row
    lane_req = iota((reqs, LANES), 1) - HD
    path_hot = (
        (lane_req == mid_col)
        & (lane_req < MIDS)
        | (lane_req - MIDS == lax.shift_right_logical(leaf_col, 3)) & (lane_req < 2 * MIDS)
        | (lane_req - 2 * MIDS == (leaf_col & 7)) & (lane_req < 3 * MIDS)
    ) & (lane_req >= 0)
    path_table = jnp.where(path_hot, 1.0, 0.0).astype(BF16)

    def requests_of(device):
        place = device * rows + iota((rows, reqs), 0)
        return (place >= start_row) & (place < end_row)

    own_hit = requests_of(blk)
    own_place = blk * rows + iota((rows, 1), 0)
    own_start = jnp.sum(jnp.where(own_hit, start_row, 0), axis=1, keepdims=True)
    position = own_place + jnp.sum(jnp.where(own_hit, shift_row, 0), axis=1, keepdims=True)
    angles = position.astype(F32) * freq_v[...]
    cosine = jnp.cos(angles)
    sine = jnp.sin(angles)
    lane = iota((rows, LANES), 1)
    first_half = lax.rem(lane, HD) < HD // 2
    sine = jnp.where(first_half, -sine, sine)
    low = lane < HD

    def rotated(v, cos, sin):
        swapped = jnp.where(
            first_half,
            pltpu.roll(v, LANES - HD // 2, 1),
            pltpu.roll(v, HD // 2, 1),
        )
        return v * cos + swapped * sin

    copies[8].wait()
    wide = tok_v[...].astype(F32)
    normed = (wide * lax.rsqrt(jnp.mean(wide * wide, axis=1, keepdims=True) + EPSILON)).astype(BF16)
    copies[9].wait()
    queries = jnp.dot(normed, wq_v[...], preferred_element_type=F32)
    for half in range(heads // 2):
        turned = rotated(queries[:, half * LANES : (half + 1) * LANES], cosine, sine)
        qbuf[0, :, half * LANES : (half + 1) * LANES] = turned.astype(BF16) * SCORE_SCALE
    for place in range(1, nz):
        q_copy(place).start()
    copies[10].wait()
    copies[11].wait()
    keys_new = jnp.dot(normed, wk_v[...], preferred_element_type=F32)
    values_new = jnp.dot(normed, wv_v[...], preferred_element_type=F32)
    pack = jnp.concatenate([keys_new, values_new], axis=1)
    pack = rotated(pack, jnp.where(low, cosine, 1.0), jnp.where(low, sine, 0.0))
    near[4] = pack.astype(BF16)
    for step in range(1, 5):
        near_copy(step).start()

    @pl.loop(0, nz)
    def _(place):
        hit = jnp.where(requests_of(z_peer(place)), 1.0, 0.0).astype(BF16)
        hot[place] = jnp.dot(hit, path_table, preferred_element_type=F32).astype(BF16)

    copies[6].wait()
    copies[7].wait()
    page_len = pages.shape[2]
    per_slot = pages.shape[1]
    lane_page = iota((page_len, LANES), 1) - HD
    slot_at = iota((page_len, LANES), 0)

    @pl.loop(0, 2 * ny)
    def _(slot):
        place = lax.div(slot, 2)
        other = lax.rem(slot, 2)
        source = blk_of(
            lax.rem(yi + offset_at(place, ny), ny), zi, core + other - 2 * core * other
        )
        for page in range(per_slot):
            node = node_s[source * per_slot + page]
            used = fill_s[source * per_slot + page]
            node = jnp.full((page_len, LANES), node, I32)
            leaf = node - 1 - MIDS
            is_mid = (node >= 1) & (leaf < 0)
            is_leaf = leaf >= 0
            bad = (
                (lane_page >= 0)
                & (lane_page < MIDS)
                & ((slot_at >= used) | (is_mid & (lane_page != node - 1)))
            )
            bad = bad | (
                is_leaf
                & (lane_page >= MIDS)
                & (lane_page < 2 * MIDS)
                & (lane_page - MIDS != lax.shift_right_arithmetic(leaf, 3))
            )
            bad = bad | (
                is_leaf
                & (lane_page >= 2 * MIDS)
                & (lane_page < 3 * MIDS)
                & (lane_page - 2 * MIDS != (leaf & 7))
            )
            at = pl.multiple_of((slot * per_slot + page) * page_len, page_len)
            keys[pl.ds(at, page_len), :] = jnp.where(bad, NEGATIVE, 0.0).astype(BF16)

    vals[HD:, :] = jnp.ones((vals.shape[0] - HD, vals.shape[1]), BF16)
    low_one = jnp.where(low[:1], 1.0, 0.0).astype(BF16)

    def build_queries(place):
        for half in range(heads // 2):
            two = qbuf[place, :, half * LANES : (half + 1) * LANES]
            turned = pltpu.roll(two.astype(F32), HD, 1).astype(BF16)
            extra = hot[place]
            base = 2 * half * rows
            qaug[place, base : base + rows, :] = two * low_one + extra
            qaug[place, base + rows : base + 2 * rows, :] = turned * low_one + extra

    slot_keys = per_slot * page_len

    def build_keys(place):
        span = slice(2 * place * slot_keys, 2 * (place + 1) * slot_keys)
        both = kvb[2 * place : 2 * place + 2].reshape(2 * slot_keys, LANES)
        keys[span, :] = both * low_one + keys[span, :]
        vals[0:HD, span] = both.astype(F32).T[HD:].astype(BF16)

    def attend(query, key, value):
        scores = lax.dot_general(key, query, (((1,), (1,)), ((), ())), preferred_element_type=F32)
        return scores, value

    def fold(scores, value):
        top = jnp.max(scores, axis=0, keepdims=True)
        weights = jnp.exp(scores - top).astype(BF16)
        return top, jnp.dot(value, weights, preferred_element_type=F32)

    half_places = ny // 2
    for place in range(1, half_places):
        kv_copy(mirror(place, ny)).wait_recv()
        forward(place).start()

    build_queries(0)

    for step in range(1, 5):
        near_copy(step).wait_recv()
    near_rows = 5 * rows
    near_all = near[...].reshape(near_rows, LANES)
    near_scores = lax.dot_general(
        near_all * low_one, qaug[0], (((1,), (1,)), ((), ())), preferred_element_type=F32
    )
    start_lane = jnp.sum(
        jnp.where(
            iota((rows, group), 0) == lax.rem(iota((rows, group), 1), rows), own_start, 0
        ),
        axis=0,
        keepdims=True,
    )
    key_place = (blk - 4) * rows + iota((near_rows, group), 0)
    row_place = blk * rows + lax.rem(iota((near_rows, group), 1), rows)
    allowed = (key_place >= start_lane) & (key_place <= row_place)
    near_scores = jnp.where(allowed, near_scores, NEGATIVE)
    near_values = jnp.concatenate(
        [near_all.astype(F32).T[HD:].astype(BF16), jnp.ones((16, near_rows), BF16)], axis=0
    )
    near_top, near_sum = fold(near_scores, near_values)
    near_total = near_sum[HD : HD + 1]
    near_out = near_sum[0:HD] / near_total
    near_lse = near_top + jnp.log(near_total)

    copies[12].wait()
    for place in range(half_places):
        forward(place).wait_recv()
        build_keys(place)
    first_keys = 2 * half_places * slot_keys
    all_keys = 2 * ny * slot_keys

    @pl.loop(0, nz)
    def _(place):
        @pl.when(place > 0)
        def _():
            q_copy(mirror(place, nz)).wait_recv()
            build_queries(place)

        scores, value = attend(qaug[place], keys[0:first_keys, :], vals[:, 0:first_keys])
        top, total = fold(scores, value)
        state_top[place] = jnp.broadcast_to(top, (8, group))
        state_sum[place] = total

        @pl.when(place >= nz - (ny - half_places))
        def _():
            line = place - nz + ny
            kv_copy(mirror(line, ny)).wait_recv()
            forward(line).start()

    for place in range(half_places, ny):
        forward(place).wait_recv()
        build_keys(place)

    @pl.loop(0, nz)
    def _(turn):
        place = nz - 1 - turn
        scores, value = attend(
            qaug[place], keys[first_keys:all_keys, :], vals[:, first_keys:all_keys]
        )
        top, total = fold(scores, value)
        old_top = state_top[place][0:1]
        new_top = jnp.maximum(top, old_top)
        total = total * jnp.exp(top - new_top) + state_sum[place] * jnp.exp(old_top - new_top)
        mass = total[HD : HD + 1]
        result = total[0:HD] / mass
        lse = jnp.broadcast_to(new_top + jnp.log(mass), (8, group))
        part[place] = result.astype(BF16)
        part_lse[place] = lse
        own_part[...] = result

        @pl.when(place > 0)
        def _():
            for copy in part_copies(place):
                copy.start()

    lses = [near_lse, part_lse[0][0:1]]
    for place in range(1, nz):
        for copy in part_copies(mirror(place, nz)):
            copy.wait_recv()
        lses.append(got_lse[place][0:1])
    top = functools.reduce(jnp.maximum, lses)
    shares = [jnp.exp(lse - top) for lse in lses]
    scale = 1.0 / functools.reduce(jnp.add, shares)
    joined = near_out * (shares[0] * scale) + own_part[...] * (shares[1] * scale)
    for place in range(1, nz):
        joined = joined + got[place].astype(F32) * (shares[place + 1] * scale)
    for half in range(heads // 2):
        two = joined[:, half * LANES : (half + 1) * LANES]
        square = jnp.concatenate([two, pltpu.roll(two, rows, 1)], axis=0)
        att[hx, :, half * LANES : (half + 1) * LANES] = square.T[0:rows].astype(BF16)
    for step in range(1, nx):
        att_copy(step).start()

    copies[13].wait()
    total = jnp.dot(att[hx], wob[hx], preferred_element_type=F32)
    for step in range(1, nx):
        wo_copy(step).wait_recv()
        att_copy(step).wait_recv()
        source = lax.rem(hx + nx - step, nx)
        total = total + jnp.dot(att[source], wob[source], preferred_element_type=F32)
    out[...] = total.astype(BF16)

    for place in range(1, ny):
        kv_copy(place).wait_send()
    for place in range(ny):
        forward(place).wait_send()
    for place in range(1, nz):
        q_copy(place).wait_send()
        for copy in part_copies(place):
            copy.wait_send()
    for step in range(1, 5):
        near_copy(step).wait_send()
    for step in range(1, nx):
        wo_copy(step).wait_send()
        att_copy(step).wait_send()


def local(
    tokens, q_weight, k_weight, v_weight, o_weight, kv_pages, page_node, page_fill, req_len, req_leaf, leaf_parent
):
    nx = lax.axis_size("head")
    ny, nz = LINES[lax.axis_size("blk")]
    rows, width = tokens.shape
    heads = q_weight.shape[1] // HD
    group = heads * rows
    out_cols = o_weight.shape[1] // nx
    per_slot, page_len = kv_pages.shape[1:3]
    slots = 2 * ny
    all_keys = slots * per_slot * page_len
    pages = page_node.shape[0]
    reqs = req_len.shape[0]
    leaves = leaf_parent.shape[0]
    half = HD // 2
    freq = np.tile(ROPE_BASE ** (-np.arange(half) / half), LANES // half)[None, :]
    dma = pltpu.SemaphoreType.DMA
    scratch = [
        pltpu.VMEM((rows, width), BF16),
        pltpu.VMEM((width, heads * HD), BF16),
        pltpu.VMEM((width, HD), BF16),
        pltpu.VMEM((width, HD), BF16),
        pltpu.SMEM((pages,), I32),
        pltpu.SMEM((pages,), I32),
        pltpu.VMEM((1, pages), I32),
        pltpu.VMEM((1, pages), I32),
        pltpu.VMEM((1, reqs), I32),
        pltpu.VMEM((1, reqs), I32),
        pltpu.VMEM((1, leaves), I32),
        pltpu.VMEM((1, LANES), F32),
        pltpu.VMEM((slots, per_slot, page_len, LANES), BF16),
        pltpu.VMEM((all_keys, LANES), BF16),
        pltpu.VMEM((HD + 16, all_keys), BF16),
        pltpu.VMEM((5, rows, LANES), BF16),
        pltpu.VMEM((nz, rows, heads * HD), BF16),
        pltpu.VMEM((nz, rows, LANES), BF16),
        pltpu.VMEM((nz, group, LANES), BF16),
        pltpu.VMEM((nz, 8, group), F32),
        pltpu.VMEM((nz, HD + 16, group), F32),
        pltpu.VMEM((nz, HD, group), BF16),
        pltpu.VMEM((nz, 8, group), F32),
        pltpu.VMEM((nz, HD, group), BF16),
        pltpu.VMEM((nz, 8, group), F32),
        pltpu.VMEM((HD, group), F32),
        pltpu.VMEM((nx, rows, heads * HD), BF16),
        pltpu.VMEM((nx, heads * HD, out_cols), BF16),
        dma((14,)),
        dma((ny,)),
        dma((ny,)),
        dma((ny,)),
        dma((ny,)),
        dma((nz,)),
        dma((nz,)),
        dma((5,)),
        dma((5,)),
        dma((nz,)),
        dma((nz,)),
        dma((nz,)),
        dma((nz,)),
        dma((nx,)),
        dma((nx,)),
        dma((nx,)),
        dma((nx,)),
    ]
    anywhere = pl.BlockSpec(memory_space=pl.ANY)
    return pl.pallas_call(
        functools.partial(kernel, (nx, ny, nz, rows, heads)),
        out_shape=jax.ShapeDtypeStruct((rows, out_cols), BF16),
        in_specs=[anywhere] * 12,
        out_specs=pl.BlockSpec(memory_space=pltpu.VMEM),
        scratch_shapes=scratch,
        compiler_params=pltpu.CompilerParams(
            collective_id=0, has_side_effects=True, vmem_limit_bytes=56 << 20
        ),
        name="tree_attention",
    )(
        tokens,
        q_weight,
        k_weight,
        v_weight,
        o_weight,
        kv_pages,
        page_node[None, :],
        page_fill[None, :],
        req_len[None, :],
        req_leaf[None, :],
        leaf_parent[None, :],
        jnp.asarray(freq, F32),
    )


def solution(mesh):
    return jax.shard_map(
        local,
        mesh=mesh,
        in_specs=(
            P("blk", None),
            P(None, "head"),
            P(None, "head"),
            P(None, "head"),
            P("head", None),
            P("head", "blk", None, None),
            P(),
            P(),
            P(),
            P(),
            P(),
        ),
        out_specs=P("blk", "head"),
        check_vma=False,
    )
```

time: 207 us -> 60.7 us (0.29); the launches traced: 205 us -> 60.5 us
  waiting for transfers between devices: 86.1 us -> 0 us
  Pallas kernels: 0 us -> 54 us
  local copies, waits for them, and re-layouts: 47 us -> 6.42 us
  matrix products: 21.1 us -> 0 us
  starting transfers between devices: 19.6 us -> 0 us
  other arithmetic: 16.3 us -> 0 us
  between operations: 13.7 us -> 0.01 us
    all_gather x1 -> x0, waiting for transfers between devices: 63.6 us -> none  [local(): shard_pages = lax.all_gather(kv_pages, 'blk', axis=1, tiled=True)]
    pallas_call x0 -> x1, Pallas kernels: none -> 54 us  [local(): pl.pallas_call(functools.partial(kernel, (nx, ny, nz, rows, heads)), out_...]
    dynamic_slice x36 -> x0, local copies, waits for them, and re-layouts: 31.1 us -> none  [the longest x12 13 us: one_group(): lax.dynamic_slice_in_dim(shard_pages, first_page, group_pages, 1)]
    reduce_scatter x1 -> x0, waiting for transfers between devices: 21.7 us -> none  [local(): lax.psum_scatter(partial_out, 'head', scatter_dimension=1, tiled=True)]
    dot_general x30 -> x0, matrix products: 21.1 us -> none  [the longest x13 8.64 us: fold_keys(): jnp.einsum('khrn,knd->khrd', weights.astype(jnp.bfloat16), values, prefer...]
    ppermute x4 -> x0, starting transfers between devices: 19.5 us -> none  [shifted(): lax.ppermute(value, axis, [(source, source + steps) for source in range(f...]
    reduce_sum x20 -> x0, other arithmetic: 10.6 us -> none  [the longest x13 6.57 us: fold_keys(): total_new = total_old * factor + jnp.sum(weights, axis=-1)]
    and x24 -> x0, local copies, waits for them, and re-layouts: 9.91 us -> none  [page_mask(): node_hit[:, :, None] & slot_live[None, :, :]]
  transfers between devices with their start and end apart: 6 -> 0, of which waited for: 2 -> 0; matrix products, arithmetic and copies ran while one was open for 6% -> 0% of each run, Pallas kernels for 0% -> 0%
where the time goes in v1:
time: 60.7 us; the launch traced here: 60.5 us
  Pallas kernels  54 us (89%)
  local copies, waits for them, and re-layouts  6.42 us (11%)
    pallas_call x1, Pallas kernels, local(): pl.pallas_call(functools.partial(kernel, (nx, ny, nz, rows, heads)), out_...  54 us
    unnamed x9, local copies, waits for them, and re-layouts  5.28 us

profile of v1, /device:TPU:1, one launch (start us, length us, event | category | flops | bytes accessed | tf_op | source)
XLA Modules:
  0.0 60.5 jit_solution(13530241548929304742)
XLA Ops:
  0.0 0.0 copy-start.1
  0.0 0.7 %copy-done.1 = s32[384]{0:T(512)S(1)} copy-done((s32[384]{0:T(512)S(1)}, s32[384]{0:T(512)}, u32[]{:S(2)}) %copy-start.1) | copy-done | bytes 1560
  0.7 0.0 copy-start.2
  0.7 0.6 broadcast_in_dim.15.node_hbm
  1.2 0.1 copy-done.2
  1.4 0.6 broadcast_in_dim.16.fill_hbm
  1.9 0.0 copy-start
  1.9 2.0 %copy.13.wk = bf16[2048,64]{1,0:T(8,128)(2,1)} copy(bf16[2048,64]{0,1:T(8,128)(2,1)} %param.14) | data formatting | bytes 524288 | tf_op args[2]
  3.9 0.0 copy-done
  3.9 1.0 %copy.14.wv = bf16[2048,64]{1,0:T(8,128)(2,1)} copy(bf16[2048,64]{0,1:T(8,128)(2,1)S(1)} %copy-done) | data formatting | bytes 524288 | tf_op args[3]
  5.0 54.0 %tree_attention.1 = bf16[64,512]{1,0:T(8,128)(2,1)} custom-call(bf16[64,2048]{1,0:T(8,128)(2,1)} %tok.1, bf16[2048,256]{1,0:T(8,128)(2,1)} %wq.1, bf16[2048,64]{1,0:T(8,128)(2,1)} %copy.13.wk, bf16[2048,64]{1,0:T(8,128)(2,1)} %copy.14.wv, bf16[256,2048]{1,0:T(8,128)(2,1)} %wo.1, bf16[1,3,64,128]{3,2,1,0:T(8,128)(2,1)} %pages.1, ...), custom_call_target="tpu_custom_call" | custom-call | tf_op jit(solution)/shard_map/tree_attention/pallas_call | solution.py:566
  59.0 1.5 %copy.16 = bf16[64,512]{1,0:T(8,128)(2,1)} copy(bf16[64,512]{1,0:T(8,128)(2,1)} %tree_attention.1) | data formatting | bytes 131072
Async XLA Ops:
  0.0 0.7 %copy-start.1 = (s32[384]{0:T(512)S(1)}, s32[384]{0:T(512)}, u32[]{:S(2)}) copy-start(s32[384]{0:T(512)} %param.18) | copy-start | bytes 4612
  0.7 0.7 %copy-start.2 = (s32[384]{0:T(512)S(1)}, s32[384]{0:T(512)}, u32[]{:S(2)}) copy-start(s32[384]{0:T(512)} %param.19) | copy-start | bytes 4612
  1.9 2.0 %copy-start = (bf16[2048,64]{0,1:T(8,128)(2,1)S(1)}, bf16[2048,64]{0,1:T(8,128)(2,1)}, u32[]{:S(2)}) copy-start(bf16[2048,64]{0,1:T(8,128)(2,1)} %param.15) | copy-start | bytes 786436

commit v2 on v1

--- a/solution.py
+++ b/solution.py
@@ -13,6 +13,7 @@
 LANES = 128
 LINES = {128: (8, 8), 8: (2, 2)}
 NEGATIVE = -1e30
+LOWEST = -3e38
 EPSILON = 1e-06
 ROPE_BASE = 10000.0
 SCORE_SCALE = 0.125
@@ -39,6 +40,9 @@
     odd = lax.rem(place, 2)
     ends = jnp.logical_or(place == 0, place == count - 1)
     return jnp.where(ends, place, place + 2 * odd - 1)
+
+
+KV_RING, Q_RING, O_RING = False, False, False
 
 
 def iota(shape, axis):
@@ -62,8 +66,7 @@
     out,
     tok_v,
     wq_v,
-    wk_v,
-    wv_v,
+    wkv_v,
     node_s,
     fill_s,
     node_v,
@@ -85,7 +88,8 @@
     part_lse,
     got,
     got_lse,
-    own_part,
+    scores_a,
+    scores_b,
     att,
     wob,
     loc,
@@ -119,6 +123,12 @@
     def blk_of(y, z, c):
         return (y * nz + z) * 2 + c
 
+    def y_next(step):
+        return blk_of(lax.rem(yi + ny + step, ny), zi, core)
+
+    def z_next(step):
+        return blk_of(yi, lax.rem(zi + nz + step, nz), core)
+
     def y_peer(place):
         return blk_of(lax.rem(yi + offset_at(place, ny), ny), zi, core)
 
@@ -127,10 +137,40 @@
 
     sibling = blk_of(yi, zi, 1 - core)
 
+    copies = [
+        pltpu.make_async_copy(src, dst, loc.at[at])
+        for at, (src, dst) in enumerate(
+            [
+                (len_hbm, len_v.at[0]),
+                (leaf_hbm, leaf_v.at[0]),
+                (parent_hbm, parent_v.at[0]),
+                (node_hbm, node_v.at[0]),
+                (fill_hbm, fill_v.at[0]),
+                (freq_hbm, freq_v),
+                (node_hbm, node_s),
+                (fill_hbm, fill_s),
+                (tok, tok_v),
+                (wq, wq_v),
+                (wk, wkv_v.at[0:HD]),
+                (wv, wkv_v.at[HD:]),
+                (pages.at[0], kvb.at[0]),
+                (wo.at[:, pl.ds(pl.multiple_of(hx * out_cols, LANES), out_cols)], wob.at[hx]),
+            ]
+        )
+    ]
+    for at in (8, 9, 10, 11, 0, 1, 2, 3, 4, 5, 6, 7, 12):
+        copies[at].start()
+
     barrier = pltpu.get_barrier_semaphore()
     greeted = [sibling]
-    greeted += [y_peer(place) for place in range(1, ny)]
-    greeted += [z_peer(place) for place in range(1, nz)]
+    if KV_RING:
+        greeted += [y_next(1), y_next(-1)]
+    else:
+        greeted += [y_peer(place) for place in range(1, ny)]
+    if Q_RING and O_RING:
+        greeted += [z_next(1), z_next(-1)]
+    else:
+        greeted += [z_peer(place) for place in range(1, nz)]
     for step in range(1, 5):
         if step < n_blk:
             greeted += [lax.rem(blk + step, n_blk), lax.rem(blk + n_blk - step, n_blk)]
@@ -141,30 +181,6 @@
             barrier, inc=1, device_id=(lax.rem(hx + step, nx), blk), device_id_type=MESH
         )
 
-    copies = [
-        pltpu.make_async_copy(src, dst, loc.at[at])
-        for at, (src, dst) in enumerate(
-            [
-                (len_hbm, len_v),
-                (leaf_hbm, leaf_v),
-                (parent_hbm, parent_v),
-                (node_hbm, node_v),
-                (fill_hbm, fill_v),
-                (freq_hbm, freq_v),
-                (node_hbm.at[0], node_s),
-                (fill_hbm.at[0], fill_s),
-                (tok, tok_v),
-                (wq, wq_v),
-                (wk, wk_v),
-                (wv, wv_v),
-                (pages.at[0], kvb.at[0]),
-                (wo.at[:, pl.ds(pl.multiple_of(hx * out_cols, LANES), out_cols)], wob.at[hx]),
-            ]
-        )
-    ]
-    for copy in copies:
-        copy.start()
-
     def remote(src, dst, send, recv, to_head, to_blk):
         return pltpu.make_async_remote_copy(
             src_ref=src,
@@ -176,14 +192,26 @@
         )
 
     def kv_copy(place):
-        back = mirror(place, ny)
-        return remote(
-            pages.at[0], kvb.at[2 * back], kv_ss.at[place], kv_rs.at[back], hx, y_peer(place)
-        )
+        if not KV_RING:
+            back = mirror(place, ny)
+            return remote(
+                pages.at[0], kvb.at[2 * back], kv_ss.at[place], kv_rs.at[back], hx, y_peer(place)
+            )
+        src = pages.at[0] if place <= 2 else kvb.at[2 * (place - 2)]
+        to = y_next(-1 if place % 2 else 1)
+        return remote(src, kvb.at[2 * place], kv_ss.at[place], kv_rs.at[place], hx, to)
 
     def forward(place):
-        src = pages.at[0] if isinstance(place, int) and place == 0 else kvb.at[2 * place]
+        src = kvb.at[2 * place] if place else pages.at[0]
         return remote(src, kvb.at[2 * place + 1], fw_ss.at[place], fw_rs.at[place], hx, sibling)
+
+    def pass_pages(hops):
+        for place in (2 * hops - 1, 2 * hops):
+            if place < ny:
+                kv_copy(place if KV_RING else mirror(place, ny)).wait_recv()
+                if KV_RING and place + 2 < ny:
+                    kv_copy(place + 2).start()
+                forward(place).start()
 
     def wo_copy(step):
         to = lax.rem(hx + step, nx)
@@ -195,17 +223,28 @@
         return remote(near.at[4], near.at[4 - step], nr_ss.at[step], nr_rs.at[step], hx, to)
 
     def q_copy(place):
-        back = mirror(place, nz)
-        return remote(
-            qbuf.at[0], qbuf.at[back], q_ss.at[place], q_rs.at[back], hx, z_peer(place)
-        )
+        if not Q_RING:
+            back = mirror(place, nz)
+            return remote(
+                qbuf.at[0], qbuf.at[back], q_ss.at[place], q_rs.at[back], hx, z_peer(place)
+            )
+        odd = lax.rem(place, 2)
+        src = qbuf.at[jnp.maximum(place - 2, 0)]
+        to = z_next(1 - 2 * odd)
+        return remote(src, qbuf.at[place], q_ss.at[place], q_rs.at[place], hx, to)
 
     def part_copies(place):
-        back = mirror(place, nz)
-        to = z_peer(place)
+        if not O_RING:
+            back = mirror(place, nz)
+            to = z_peer(place)
+            return (
+                remote(part.at[place], got.at[back], o_ss.at[place], o_rs.at[back], hx, to),
+                remote(part_lse.at[place], got_lse.at[back], l_ss.at[place], l_rs.at[back], hx, to),
+            )
+        to = z_next(2 * lax.rem(place, 2) - 1)
         return (
-            remote(part.at[place], got.at[back], o_ss.at[place], o_rs.at[back], hx, to),
-            remote(part_lse.at[place], got_lse.at[back], l_ss.at[place], l_rs.at[back], hx, to),
+            remote(part.at[place], got.at[place], o_ss.at[place], o_rs.at[place], hx, to),
+            remote(part_lse.at[place], got_lse.at[place], l_ss.at[place], l_rs.at[place], hx, to),
         )
 
     def att_copy(step):
@@ -213,11 +252,10 @@
         return remote(att.at[hx], att.at[hx], a_ss.at[step], a_rs.at[step], to, blk)
 
     pl.semaphore_wait(barrier, len(greeted) + nx - 1)
-    for place in range(1, ny):
-        kv_copy(place).start()
+    for place in (1, 2) if KV_RING else range(1, ny):
+        if place < ny:
+            kv_copy(place).start()
     forward(0).start()
-    for step in range(1, nx):
-        wo_copy(step).start()
 
     for copy in copies[:6]:
         copy.wait()
@@ -276,6 +314,8 @@
         )
         return v * cos + swapped * sin
 
+    pass_pages(1)
+
     copies[8].wait()
     wide = tok_v[...].astype(F32)
     normed = (wide * lax.rsqrt(jnp.mean(wide * wide, axis=1, keepdims=True) + EPSILON)).astype(BF16)
@@ -284,21 +324,27 @@
     for half in range(heads // 2):
         turned = rotated(queries[:, half * LANES : (half + 1) * LANES], cosine, sine)
         qbuf[0, :, half * LANES : (half + 1) * LANES] = turned.astype(BF16) * SCORE_SCALE
-    for place in range(1, nz):
-        q_copy(place).start()
+    for place in (1, 2) if Q_RING else range(1, nz):
+        if place < nz:
+            q_copy(place).start()
     copies[10].wait()
     copies[11].wait()
-    keys_new = jnp.dot(normed, wk_v[...], preferred_element_type=F32)
-    values_new = jnp.dot(normed, wv_v[...], preferred_element_type=F32)
-    pack = jnp.concatenate([keys_new, values_new], axis=1)
+    pack = lax.dot_general(
+        normed, wkv_v[...], (((1,), (1,)), ((), ())), preferred_element_type=F32
+    )
     pack = rotated(pack, jnp.where(low, cosine, 1.0), jnp.where(low, sine, 0.0))
     near[4] = pack.astype(BF16)
     for step in range(1, 5):
         near_copy(step).start()
+    copies[13].start()
+    for step in range(1, nx):
+        wo_copy(step).start()
+
+    pass_pages(2)
 
     @pl.loop(0, nz)
     def _(place):
-        hit = jnp.where(requests_of(z_peer(place)), 1.0, 0.0).astype(BF16)
+        hit = jnp.where(requests_of(z_next(offset_at(place, nz))), 1.0, 0.0).astype(BF16)
         hot[place] = jnp.dot(hit, path_table, preferred_element_type=F32).astype(BF16)
 
     copies[6].wait()
@@ -362,21 +408,136 @@
         keys[span, :] = both * low_one + keys[span, :]
         vals[0:HD, span] = both.astype(F32).T[HD:].astype(BF16)
 
-    def attend(query, key, value):
-        scores = lax.dot_general(key, query, (((1,), (1,)), ((), ())), preferred_element_type=F32)
-        return scores, value
-
     def fold(scores, value):
         top = jnp.max(scores, axis=0, keepdims=True)
         weights = jnp.exp(scores - top).astype(BF16)
         return top, jnp.dot(value, weights, preferred_element_type=F32)
 
+    pass_pages(3)
     half_places = ny // 2
-    for place in range(1, half_places):
-        kv_copy(mirror(place, ny)).wait_recv()
-        forward(place).start()
-
     build_queries(0)
+
+    copies[12].wait()
+    for place in range(half_places):
+        forward(place).wait_recv()
+        build_keys(place)
+    span_keys = 2 * half_places * slot_keys
+    tile = 512 if span_keys % 512 == 0 else 384
+    tiles = range(0, span_keys, tile)
+
+    def item(index):
+        half = lax.div(index, nz)
+        at = lax.rem(index, nz)
+        place = half * (nz - 1 - at) + (1 - half) * at
+        return place, pl.multiple_of(half * span_keys, LANES)
+
+    def score(index, into, at, top):
+        place, first = item(index)
+        found = lax.dot_general(
+            keys[pl.ds(first + at, tile), :],
+            qaug[place],
+            (((1,), (1,)), ((), ())),
+            preferred_element_type=F32,
+        )
+        into[pl.ds(at, tile), :] = found
+        best = jnp.max(found.reshape(tile // 8, 8, group), axis=0)
+        return best if top is None else jnp.maximum(top, best)
+
+    def step_item(index, held, following, into, top):
+        place, first = item(index)
+        best = total = None
+        for at in tiles:
+            best = score(following, into, at, best)
+            weights = jnp.exp(held[pl.ds(at, tile), :] - top).astype(BF16)
+            more = jnp.dot(
+                vals[:, pl.ds(first + at, tile)], weights, preferred_element_type=F32
+            )
+            total = more if total is None else total + more
+        old_top = state_top[place]
+        new_top = jnp.maximum(top, old_top)
+        total = total * jnp.exp(top - new_top) + state_sum[place] * jnp.exp(old_top - new_top)
+        state_sum[place] = total
+        state_top[place] = new_top
+        return jnp.max(best, axis=0, keepdims=True)
+
+    def finish(index):
+        place, _ = item(index)
+
+        @pl.when((index >= nz) & (place > 0))
+        def _():
+            total = state_sum[place]
+            if not O_RING:
+                mass = total[HD : HD + 1]
+                part[place] = (total[0:HD] * (1.0 / mass)).astype(BF16)
+                part_lse[place] = state_top[place] + jnp.log(mass)
+                for copy in part_copies(place):
+                    copy.start()
+                return
+
+            @pl.when(place + 2 < nz)
+            def _():
+                for copy in part_copies(place + 2):
+                    copy.wait_recv()
+
+            own_top = state_top[place]
+            far_top = got_lse[place + 2]
+            top = jnp.maximum(own_top, far_top)
+            own_scale = jnp.exp(own_top - top)
+            far_scale = jnp.exp(far_top - top)
+            mass = total[HD : HD + 1] * own_scale + far_scale
+            share = 1.0 / mass
+            result = total[0:HD] * (own_scale * share)
+            result = result + got[place + 2].astype(F32) * (far_scale * share)
+            part[place] = result.astype(BF16)
+            part_lse[place] = top + jnp.log(mass)
+            for copy in part_copies(place):
+                copy.start()
+
+    state_top[...] = jnp.full(state_top.shape, LOWEST, F32)
+    state_sum[...] = jnp.zeros(state_sum.shape, F32)
+    for place in (nz, nz + 1):
+        got_lse[place] = jnp.full((1, group), NEGATIVE, F32)
+        got[place] = jnp.zeros((HD, group), BF16)
+    items = 2 * nz
+
+    def two_items(turn, top):
+        for hops in range(4, ny // 2 + 1):
+
+            @pl.when(turn == hops - 3)
+            def _():
+                pass_pages(hops)
+
+        for ahead in (1, 2):
+            place = 2 * turn + ahead
+
+            @pl.when(place < nz)
+            def _():
+                q_copy(place if Q_RING else mirror(place, nz)).wait_recv()
+                if Q_RING:
+
+                    @pl.when(place + 2 < nz)
+                    def _():
+                        q_copy(place + 2).start()
+
+                build_queries(place)
+
+            @pl.when(place == nz)
+            def _():
+                for line in range(half_places, ny):
+                    forward(line).wait_recv()
+                    build_keys(line)
+
+        index = 2 * turn
+        top = step_item(index, scores_a, index + 1, scores_b, top)
+        finish(index)
+        top = step_item(index + 1, scores_b, jnp.minimum(index + 2, items - 1), scores_a, top)
+        finish(index + 1)
+        return top
+
+    best = None
+    for at in tiles:
+        best = score(0, scores_a, at, best)
+    lax.fori_loop(0, nz, two_items, jnp.max(best, axis=0, keepdims=True))
 
     for step in range(1, 5):
         near_copy(step).wait_recv()
@@ -404,67 +565,20 @@
     near_out = near_sum[0:HD] / near_total
     near_lse = near_top + jnp.log(near_total)
 
-    copies[12].wait()
-    for place in range(half_places):
-        forward(place).wait_recv()
-        build_keys(place)
-    first_keys = 2 * half_places * slot_keys
-    all_keys = 2 * ny * slot_keys
-
-    @pl.loop(0, nz)
-    def _(place):
-        @pl.when(place > 0)
-        def _():
-            q_copy(mirror(place, nz)).wait_recv()
-            build_queries(place)
-
-        scores, value = attend(qaug[place], keys[0:first_keys, :], vals[:, 0:first_keys])
-        top, total = fold(scores, value)
-        state_top[place] = jnp.broadcast_to(top, (8, group))
-        state_sum[place] = total
-
-        @pl.when(place >= nz - (ny - half_places))
-        def _():
-            line = place - nz + ny
-            kv_copy(mirror(line, ny)).wait_recv()
-            forward(line).start()
-
-    for place in range(half_places, ny):
-        forward(place).wait_recv()
-        build_keys(place)
-
-    @pl.loop(0, nz)
-    def _(turn):
-        place = nz - 1 - turn
-        scores, value = attend(
-            qaug[place], keys[first_keys:all_keys, :], vals[:, first_keys:all_keys]
-        )
-        top, total = fold(scores, value)
-        old_top = state_top[place][0:1]
-        new_top = jnp.maximum(top, old_top)
-        total = total * jnp.exp(top - new_top) + state_sum[place] * jnp.exp(old_top - new_top)
-        mass = total[HD : HD + 1]
-        result = total[0:HD] / mass
-        lse = jnp.broadcast_to(new_top + jnp.log(mass), (8, group))
-        part[place] = result.astype(BF16)
-        part_lse[place] = lse
-        own_part[...] = result
-
-        @pl.when(place > 0)
-        def _():
-            for copy in part_copies(place):
-                copy.start()
-
-    lses = [near_lse, part_lse[0][0:1]]
-    for place in range(1, nz):
-        for copy in part_copies(mirror(place, nz)):
-            copy.wait_recv()
-        lses.append(got_lse[place][0:1])
+    own_sum = state_sum[0]
+    own_total = own_sum[HD : HD + 1]
+    lses = [near_lse, state_top[0] + jnp.log(own_total)]
+    for place in (1, 2) if O_RING else range(1, nz):
+        if place < nz:
+            for copy in part_copies(place if O_RING else mirror(place, nz)):
+                copy.wait_recv()
+            lses.append(got_lse[place])
     top = functools.reduce(jnp.maximum, lses)
     shares = [jnp.exp(lse - top) for lse in lses]
     scale = 1.0 / functools.reduce(jnp.add, shares)
-    joined = near_out * (shares[0] * scale) + own_part[...] * (shares[1] * scale)
-    for place in range(1, nz):
+    joined = near_out * (shares[0] * scale)
+    joined = joined + own_sum[0:HD] * (shares[1] * scale / own_total)
+    for place in range(1, len(lses) - 1):
         joined = joined + got[place].astype(F32) * (shares[place + 1] * scale)
     for half in range(heads // 2):
         two = joined[:, half * LANES : (half + 1) * LANES]
@@ -518,8 +632,7 @@
     scratch = [
         pltpu.VMEM((rows, width), BF16),
         pltpu.VMEM((width, heads * HD), BF16),
-        pltpu.VMEM((width, HD), BF16),
-        pltpu.VMEM((width, HD), BF16),
+        pltpu.VMEM((2 * HD, width), BF16),
         pltpu.SMEM((pages,), I32),
         pltpu.SMEM((pages,), I32),
         pltpu.VMEM((1, pages), I32),
@@ -535,13 +648,14 @@
         pltpu.VMEM((nz, rows, heads * HD), BF16),
         pltpu.VMEM((nz, rows, LANES), BF16),
         pltpu.VMEM((nz, group, LANES), BF16),
-        pltpu.VMEM((nz, 8, group), F32),
+        pltpu.VMEM((nz, 1, group), F32),
         pltpu.VMEM((nz, HD + 16, group), F32),
         pltpu.VMEM((nz, HD, group), BF16),
-        pltpu.VMEM((nz, 8, group), F32),
-        pltpu.VMEM((nz, HD, group), BF16),
-        pltpu.VMEM((nz, 8, group), F32),
-        pltpu.VMEM((HD, group), F32),
+        pltpu.VMEM((nz, 1, group), F32),
+        pltpu.VMEM((nz + 2, HD, group), BF16),
+        pltpu.VMEM((nz + 2, 1, group), F32),
+        pltpu.VMEM((all_keys // 2, group), F32),
+        pltpu.VMEM((all_keys // 2, group), F32),
         pltpu.VMEM((nx, rows, heads * HD), BF16),
         pltpu.VMEM((nx, heads * HD, out_cols), BF16),
         dma((14,)),
@@ -576,15 +690,15 @@
     )(
         tokens,
         q_weight,
-        k_weight,
-        v_weight,
+        k_weight.T,
+        v_weight.T,
         o_weight,
         kv_pages,
-        page_node[None, :],
-        page_fill[None, :],
-        req_len[None, :],
-        req_leaf[None, :],
-        leaf_parent[None, :],
+        page_node,
+        page_fill,
+        req_len,
+        req_leaf,
+        leaf_parent,
         jnp.asarray(freq, F32),
     )
 

time: 60.7 us -> 47.2 us (0.78)
  Pallas kernels: 54 us -> 45.4 us
  local copies, waits for them, and re-layouts: 6.42 us -> 1.47 us
    pallas_call x1, Pallas kernels: 54 us -> 45.4 us  [local(): pl.pallas_call(functools.partial(kernel, (nx, ny, nz, rows, heads)), out_...]
    unnamed x9 -> x1, local copies, waits for them, and re-layouts: 5.28 us -> 1.47 us
    broadcast_in_dim x2 -> x0, local copies, waits for them, and re-layouts: 1.14 us -> none  [the longest x1 0.58 us: local(): page_fill[None, :]]
where the time goes in v2:
time: 47.2 us; the launch traced here: 46.8 us
  Pallas kernels  45.4 us (96%)
  local copies, waits for them, and re-layouts  1.47 us (3%)
    pallas_call x1, Pallas kernels, local(): pl.pallas_call(functools.partial(kernel, (nx, ny, nz, rows, heads)), out_...  45.4 us
    unnamed x1, local copies, waits for them, and re-layouts  1.47 us

profile of v2, /device:TPU:1, one launch (start us, length us, event | category | flops | bytes accessed | tf_op | source)
XLA Modules:
  0.0 46.8 jit_solution(17923037388670632120)
XLA Ops:
  0.0 45.4 %tree_attention.1 = bf16[64,512]{1,0:T(8,128)(2,1)} custom-call(bf16[64,2048]{1,0:T(8,128)(2,1)} %tok.1, bf16[2048,256]{1,0:T(8,128)(2,1)} %wq.1, bf16[64,2048]{1,0:T(8,128)(2,1)} %bitcast.2, bf16[64,2048]{1,0:T(8,128)(2,1)} %bitcast.3, bf16[256,2048]{1,0:T(8,128)(2,1)} %wo.1, bf16[1,3,64,128]{3,2,1,0:T(8,128)(2,1)} %pages.1, s32[384]{0:T(512)} %node_hbm.1, ...), custom_call_target="tpu_custom_call" | custom-call | tf_op jit(solution)/shard_map/tree_attention/pallas_call | solution.py:680
  45.4 1.5 %copy.14 = bf16[64,512]{1,0:T(8,128)(2,1)} copy(bf16[64,512]{1,0:T(8,128)(2,1)} %tree_attention.1) | data formatting | bytes 131072

commit v3 on v2

--- a/solution.py
+++ b/solution.py
@@ -40,9 +40,6 @@
     odd = lax.rem(place, 2)
     ends = jnp.logical_or(place == 0, place == count - 1)
     return jnp.where(ends, place, place + 2 * odd - 1)
-
-
-KV_RING, Q_RING, O_RING = False, False, False
 
 
 def iota(shape, axis):
@@ -63,7 +60,8 @@
     leaf_hbm,
     parent_hbm,
     freq_hbm,
-    out,
+    att,
+    wob,
     tok_v,
     wq_v,
     wkv_v,
@@ -90,8 +88,7 @@
     got_lse,
     scores_a,
     scores_b,
-    att,
-    wob,
+    own_att,
     loc,
     kv_ss,
     kv_rs,
@@ -112,7 +109,8 @@
 ):
     nx, ny, nz, rows, heads = sizes
     group = heads * rows
-    out_cols = out.shape[1]
+    out_cols = wob.shape[1]
+    width = heads * HD
     n_blk = ny * nz * 2
     hx = lax.axis_index("head")
     blk = lax.axis_index("blk")
@@ -123,12 +121,6 @@
     def blk_of(y, z, c):
         return (y * nz + z) * 2 + c
 
-    def y_next(step):
-        return blk_of(lax.rem(yi + ny + step, ny), zi, core)
-
-    def z_next(step):
-        return blk_of(yi, lax.rem(zi + nz + step, nz), core)
-
     def y_peer(place):
         return blk_of(lax.rem(yi + offset_at(place, ny), ny), zi, core)
 
@@ -137,6 +129,7 @@
 
     sibling = blk_of(yi, zi, 1 - core)
 
+    my_rows = pl.ds(pl.multiple_of(hx * width, LANES), width)
     copies = [
         pltpu.make_async_copy(src, dst, loc.at[at])
         for at, (src, dst) in enumerate(
@@ -154,7 +147,7 @@
                 (wk, wkv_v.at[0:HD]),
                 (wv, wkv_v.at[HD:]),
                 (pages.at[0], kvb.at[0]),
-                (wo.at[:, pl.ds(pl.multiple_of(hx * out_cols, LANES), out_cols)], wob.at[hx]),
+                (wo.at[:, pl.ds(pl.multiple_of(hx * out_cols, LANES), out_cols)], wob.at[my_rows]),
             ]
         )
     ]
@@ -162,15 +155,11 @@
         copies[at].start()
 
     barrier = pltpu.get_barrier_semaphore()
-    greeted = [sibling]
-    if KV_RING:
-        greeted += [y_next(1), y_next(-1)]
-    else:
-        greeted += [y_peer(place) for place in range(1, ny)]
-    if Q_RING and O_RING:
-        greeted += [z_next(1), z_next(-1)]
-    else:
-        greeted += [z_peer(place) for place in range(1, nz)]
+    greeted = []
+    for place in range(max(ny, nz) - 1, 0, -1):
+        greeted += [y_peer(place)] if place < ny else []
+        greeted += [z_peer(place)] if place < nz else []
+    greeted.append(sibling)
     for step in range(1, 5):
         if step < n_blk:
             greeted += [lax.rem(blk + step, n_blk), lax.rem(blk + n_blk - step, n_blk)]
@@ -192,69 +181,50 @@
         )
 
     def kv_copy(place):
-        if not KV_RING:
-            back = mirror(place, ny)
-            return remote(
-                pages.at[0], kvb.at[2 * back], kv_ss.at[place], kv_rs.at[back], hx, y_peer(place)
-            )
-        src = pages.at[0] if place <= 2 else kvb.at[2 * (place - 2)]
-        to = y_next(-1 if place % 2 else 1)
-        return remote(src, kvb.at[2 * place], kv_ss.at[place], kv_rs.at[place], hx, to)
+        back = mirror(place, ny)
+        return remote(
+            pages.at[0], kvb.at[back], kv_ss.at[place], kv_rs.at[back], hx, y_peer(place)
+        )
 
     def forward(place):
-        src = kvb.at[2 * place] if place else pages.at[0]
-        return remote(src, kvb.at[2 * place + 1], fw_ss.at[place], fw_rs.at[place], hx, sibling)
-
-    def pass_pages(hops):
-        for place in (2 * hops - 1, 2 * hops):
-            if place < ny:
-                kv_copy(place if KV_RING else mirror(place, ny)).wait_recv()
-                if KV_RING and place + 2 < ny:
-                    kv_copy(place + 2).start()
-                forward(place).start()
+        src = kvb.at[place] if place else pages.at[0]
+        return remote(src, kvb.at[ny + place], fw_ss.at[place], fw_rs.at[place], hx, sibling)
+
+    def pass_pages(place):
+        kv_copy(mirror(place, ny)).wait_recv()
+        forward(place).start()
 
     def wo_copy(step):
         to = lax.rem(hx + step, nx)
         cols = pl.ds(pl.multiple_of(to * out_cols, LANES), out_cols)
-        return remote(wo.at[:, cols], wob.at[hx], w_ss.at[step], w_rs.at[step], to, blk)
+        return remote(wo.at[:, cols], wob.at[my_rows], w_ss.at[step], w_rs.at[step], to, blk)
 
     def near_copy(step):
         to = lax.rem(blk + step, n_blk)
         return remote(near.at[4], near.at[4 - step], nr_ss.at[step], nr_rs.at[step], hx, to)
 
     def q_copy(place):
-        if not Q_RING:
-            back = mirror(place, nz)
-            return remote(
-                qbuf.at[0], qbuf.at[back], q_ss.at[place], q_rs.at[back], hx, z_peer(place)
-            )
-        odd = lax.rem(place, 2)
-        src = qbuf.at[jnp.maximum(place - 2, 0)]
-        to = z_next(1 - 2 * odd)
-        return remote(src, qbuf.at[place], q_ss.at[place], q_rs.at[place], hx, to)
+        back = mirror(place, nz)
+        return remote(
+            qbuf.at[0], qbuf.at[back], q_ss.at[place], q_rs.at[back], hx, z_peer(place)
+        )
 
     def part_copies(place):
-        if not O_RING:
-            back = mirror(place, nz)
-            to = z_peer(place)
-            return (
-                remote(part.at[place], got.at[back], o_ss.at[place], o_rs.at[back], hx, to),
-                remote(part_lse.at[place], got_lse.at[back], l_ss.at[place], l_rs.at[back], hx, to),
-            )
-        to = z_next(2 * lax.rem(place, 2) - 1)
+        back = mirror(place, nz)
+        to = z_peer(place)
         return (
-            remote(part.at[place], got.at[place], o_ss.at[place], o_rs.at[place], hx, to),
-            remote(part_lse.at[place], got_lse.at[place], l_ss.at[place], l_rs.at[place], hx, to),
+            remote(part.at[place], got.at[back], o_ss.at[place], o_rs.at[back], hx, to),
+            remote(part_lse.at[place], got_lse.at[back], l_ss.at[place], l_rs.at[back], hx, to),
         )
 
     def att_copy(step):
         to = lax.rem(hx + step, nx)
-        return remote(att.at[hx], att.at[hx], a_ss.at[step], a_rs.at[step], to, blk)
+        return remote(own_att, att.at[:, my_rows], a_ss.at[step], a_rs.at[step], to, blk)
 
     pl.semaphore_wait(barrier, len(greeted) + nx - 1)
-    for place in (1, 2) if KV_RING else range(1, ny):
-        if place < ny:
-            kv_copy(place).start()
+    half_places = ny // 2
+    for place in range(1, half_places):
+        kv_copy(mirror(place, ny)).start()
     forward(0).start()
 
     for copy in copies[:6]:
@@ -314,8 +284,6 @@
         )
         return v * cos + swapped * sin
 
-    pass_pages(1)
-
     copies[8].wait()
     wide = tok_v[...].astype(F32)
     normed = (wide * lax.rsqrt(jnp.mean(wide * wide, axis=1, keepdims=True) + EPSILON)).astype(BF16)
@@ -324,9 +292,10 @@
     for half in range(heads // 2):
         turned = rotated(queries[:, half * LANES : (half + 1) * LANES], cosine, sine)
         qbuf[0, :, half * LANES : (half + 1) * LANES] = turned.astype(BF16) * SCORE_SCALE
-    for place in (1, 2) if Q_RING else range(1, nz):
-        if place < nz:
-            q_copy(place).start()
+    for place in range(1, nz):
+        q_copy(place).start()
+    for place in range(half_places, ny):
+        kv_copy(mirror(place, ny)).start()
     copies[10].wait()
     copies[11].wait()
     pack = lax.dot_general(
@@ -340,11 +309,9 @@
     for step in range(1, nx):
         wo_copy(step).start()
 
-    pass_pages(2)
-
     @pl.loop(0, nz)
     def _(place):
-        hit = jnp.where(requests_of(z_next(offset_at(place, nz))), 1.0, 0.0).astype(BF16)
+        hit = jnp.where(requests_of(z_peer(place)), 1.0, 0.0).astype(BF16)
         hot[place] = jnp.dot(hit, path_table, preferred_element_type=F32).astype(BF16)
 
     copies[6].wait()
@@ -356,8 +323,11 @@
 
     @pl.loop(0, 2 * ny)
     def _(slot):
-        place = lax.div(slot, 2)
-        other = lax.rem(slot, 2)
+        place = lax.rem(slot, ny)
+        other = lax.div(slot, ny)
+        pair = lax.div(slot, 2)
+        turned = jnp.where(pair == ny // 2 - 1, 1, jnp.where(pair == ny // 2, -1, 0))
+        spot = slot + 2 * turned
         source = blk_of(
             lax.rem(yi + offset_at(place, ny), ny), zi, core + other - 2 * core * other
         )
@@ -385,7 +355,7 @@
                 & (lane_page < 3 * MIDS)
                 & (lane_page - 2 * MIDS != (leaf & 7))
             )
-            at = pl.multiple_of((slot * per_slot + page) * page_len, page_len)
+            at = pl.multiple_of((spot * per_slot + page) * page_len, page_len)
             keys[pl.ds(at, page_len), :] = jnp.where(bad, NEGATIVE, 0.0).astype(BF16)
 
     vals[HD:, :] = jnp.ones((vals.shape[0] - HD, vals.shape[1]), BF16)
@@ -402,9 +372,10 @@
 
     slot_keys = per_slot * page_len
 
-    def build_keys(place):
-        span = slice(2 * place * slot_keys, 2 * (place + 1) * slot_keys)
-        both = kvb[2 * place : 2 * place + 2].reshape(2 * slot_keys, LANES)
+    def build_keys(pair):
+        spot = {ny // 2 - 1: ny // 2, ny // 2: ny // 2 - 1}.get(pair, pair)
+        span = slice(2 * spot * slot_keys, 2 * (spot + 1) * slot_keys)
+        both = kvb[2 * pair : 2 * pair + 2].reshape(2 * slot_keys, LANES)
         keys[span, :] = both * low_one + keys[span, :]
         vals[0:HD, span] = both.astype(F32).T[HD:].astype(BF16)
 
@@ -413,14 +384,20 @@
         weights = jnp.exp(scores - top).astype(BF16)
         return top, jnp.dot(value, weights, preferred_element_type=F32)
 
-    pass_pages(3)
-    half_places = ny // 2
     build_queries(0)
+    for place in range(1, ny - 2):
+        pass_pages(place)
 
     copies[12].wait()
-    for place in range(half_places):
-        forward(place).wait_recv()
-        build_keys(place)
+    for pair in range(half_places - 1):
+        build_keys(pair)
+    for place in (0, 1):
+        if place < ny - 2:
+            forward(place).wait_recv()
+        elif place < ny:
+            pass_pages(place) if place else None
+            forward(place).wait_recv()
+    build_keys(half_places)
     span_keys = 2 * half_places * slot_keys
     tile = 512 if span_keys % 512 == 0 else 384
     tiles = range(0, span_keys, tile)
@@ -466,70 +443,43 @@
         @pl.when((index >= nz) & (place > 0))
         def _():
             total = state_sum[place]
-            if not O_RING:
-                mass = total[HD : HD + 1]
-                part[place] = (total[0:HD] * (1.0 / mass)).astype(BF16)
-                part_lse[place] = state_top[place] + jnp.log(mass)
-                for copy in part_copies(place):
-                    copy.start()
-                return
-
-            @pl.when(place + 2 < nz)
-            def _():
-                for copy in part_copies(place + 2):
-                    copy.wait_recv()
-
-            own_top = state_top[place]
-            far_top = got_lse[place + 2]
-            top = jnp.maximum(own_top, far_top)
-            own_scale = jnp.exp(own_top - top)
-            far_scale = jnp.exp(far_top - top)
-            mass = total[HD : HD + 1] * own_scale + far_scale
-            share = 1.0 / mass
-            result = total[0:HD] * (own_scale * share)
-            result = result + got[place + 2].astype(F32) * (far_scale * share)
-            part[place] = result.astype(BF16)
-            part_lse[place] = top + jnp.log(mass)
+            mass = total[HD : HD + 1]
+            part[place] = (total[0:HD] * (1.0 / mass)).astype(BF16)
+            part_lse[place] = state_top[place] + jnp.log(mass)
             for copy in part_copies(place):
                 copy.start()
 
     state_top[...] = jnp.full(state_top.shape, LOWEST, F32)
     state_sum[...] = jnp.zeros(state_sum.shape, F32)
-    for place in (nz, nz + 1):
-        got_lse[place] = jnp.full((1, group), NEGATIVE, F32)
-        got[place] = jnp.zeros((HD, group), BF16)
     items = 2 * nz
 
+    def fetch(place):
+        @pl.when(place < nz)
+        def _():
+            q_copy(mirror(place, nz)).wait_recv()
+            build_queries(place)
+
     def two_items(turn, top):
-        for hops in range(4, ny // 2 + 1):
-
-            @pl.when(turn == hops - 3)
+        for line in range(max(2, ny - 2), ny):
+
+            @pl.when(turn == max(0, nz // 2 - 2))
             def _():
-                pass_pages(hops)
-
-        for ahead in (1, 2):
-            place = 2 * turn + ahead
-
-            @pl.when(place < nz)
-            def _():
-                q_copy(place if Q_RING else mirror(place, nz)).wait_recv()
-                if Q_RING:
-
-                    @pl.when(place + 2 < nz)
-                    def _():
-                        q_copy(place + 2).start()
-
-                build_queries(place)
-
-            @pl.when(place == nz)
-            def _():
-                for line in range(half_places, ny):
-                    forward(line).wait_recv()
-                    build_keys(line)
+                pass_pages(line)
 
         index = 2 * turn
+        fetch(index + 1)
         top = step_item(index, scores_a, index + 1, scores_b, top)
         finish(index)
+        fetch(index + 2)
+
+        @pl.when(index + 2 == nz)
+        def _():
+            build_keys(half_places - 1)
+            for line in range(2, ny):
+                forward(line).wait_recv()
+                if line % 2:
+                    build_keys(half_places + line // 2)
+
         top = step_item(index + 1, scores_b, jnp.minimum(index + 2, items - 1), scores_a, top)
         finish(index + 1)
         return top
@@ -568,11 +518,10 @@
     own_sum = state_sum[0]
     own_total = own_sum[HD : HD + 1]
     lses = [near_lse, state_top[0] + jnp.log(own_total)]
-    for place in (1, 2) if O_RING else range(1, nz):
-        if place < nz:
-            for copy in part_copies(place if O_RING else mirror(place, nz)):
-                copy.wait_recv()
-            lses.append(got_lse[place])
+    for place in range(1, nz):
+        for copy in part_copies(mirror(place, nz)):
+            copy.wait_recv()
+        lses.append(got_lse[place])
     top = functools.reduce(jnp.maximum, lses)
     shares = [jnp.exp(lse - top) for lse in lses]
     scale = 1.0 / functools.reduce(jnp.add, shares)
@@ -583,18 +532,17 @@
     for half in range(heads // 2):
         two = joined[:, half * LANES : (half + 1) * LANES]
         square = jnp.concatenate([two, pltpu.roll(two, rows, 1)], axis=0)
-        att[hx, :, half * LANES : (half + 1) * LANES] = square.T[0:rows].astype(BF16)
+        own_att[:, half * LANES : (half + 1) * LANES] = square.T[0:rows].astype(BF16)
     for step in range(1, nx):
         att_copy(step).start()
 
+    own_copy = pltpu.make_async_copy(own_att, att.at[:, my_rows], loc.at[14])
+    own_copy.start()
     copies[13].wait()
-    total = jnp.dot(att[hx], wob[hx], preferred_element_type=F32)
+    own_copy.wait()
     for step in range(1, nx):
         wo_copy(step).wait_recv()
         att_copy(step).wait_recv()
-        source = lax.rem(hx + nx - step, nx)
-        total = total + jnp.dot(att[source], wob[source], preferred_element_type=F32)
-    out[...] = total.astype(BF16)
 
     for place in range(1, ny):
         kv_copy(place).wait_send()
@@ -652,13 +600,12 @@
         pltpu.VMEM((nz, HD + 16, group), F32),
         pltpu.VMEM((nz, HD, group), BF16),
         pltpu.VMEM((nz, 1, group), F32),
-        pltpu.VMEM((nz + 2, HD, group), BF16),
-        pltpu.VMEM((nz + 2, 1, group), F32),
+        pltpu.VMEM((nz, HD, group), BF16),
+        pltpu.VMEM((nz, 1, group), F32),
         pltpu.VMEM((all_keys // 2, group), F32),
         pltpu.VMEM((all_keys // 2, group), F32),
-        pltpu.VMEM((nx, rows, heads * HD), BF16),
-        pltpu.VMEM((nx, heads * HD, out_cols), BF16),
-        dma((14,)),
+        pltpu.VMEM((rows, heads * HD), BF16),
+        dma((15,)),
         dma((ny,)),
         dma((ny,)),
         dma((ny,)),
@@ -677,11 +624,14 @@
         dma((nx,)),
     ]
     anywhere = pl.BlockSpec(memory_space=pl.ANY)
-    return pl.pallas_call(
+    attended, columns = pl.pallas_call(
         functools.partial(kernel, (nx, ny, nz, rows, heads)),
-        out_shape=jax.ShapeDtypeStruct((rows, out_cols), BF16),
+        out_shape=[
+            jax.ShapeDtypeStruct((rows, nx * heads * HD), BF16),
+            jax.ShapeDtypeStruct((nx * heads * HD, out_cols), BF16),
+        ],
         in_specs=[anywhere] * 12,
-        out_specs=pl.BlockSpec(memory_space=pltpu.VMEM),
+        out_specs=[anywhere, anywhere],
         scratch_shapes=scratch,
         compiler_params=pltpu.CompilerParams(
             collective_id=0, has_side_effects=True, vmem_limit_bytes=56 << 20
@@ -701,6 +651,7 @@
         leaf_parent,
         jnp.asarray(freq, F32),
     )
+    return jnp.dot(attended, columns, preferred_element_type=F32).astype(BF16)
 
 
 def solution(mesh):

time: 47.2 us -> 46.4 us (0.983)
  matrix products: 0 us -> 2.23 us
  Pallas kernels: 45.4 us -> 43.4 us
  local copies, waits for them, and re-layouts: 1.47 us -> 0 us
    dot_general x0 -> x1, matrix products: none -> 2.23 us  [local(): return jnp.dot(attended, columns, preferred_element_type=F32).astype(BF16)]
    pallas_call x1, Pallas kernels: 45.4 us -> 43.4 us  [local(): pl.pallas_call(functools.partial(kernel, (nx, ny, nz, rows, heads)), out_...]
    unnamed x1 -> x0, local copies, waits for them, and re-layouts: 1.47 us -> none
where the time goes in v3:
time: 46.4 us; the launch traced here: 45.6 us
  Pallas kernels  43.4 us (94%)
  matrix products  2.23 us (5%)
    pallas_call x1, Pallas kernels, local(): pl.pallas_call(functools.partial(kernel, (nx, ny, nz, rows, heads)), out_...  43.4 us
    dot_general x1, matrix products, local(): return jnp.dot(attended, columns, preferred_element_type=F32).astype(BF16)  2.23 us

profile of v3, /device:TPU:1, one launch (start us, length us, event | category | flops | bytes accessed | tf_op | source)
XLA Modules:
  0.0 45.6 jit_solution(17544295677155791939)
XLA Ops:
  0.0 43.4 %tree_attention.1 = (bf16[64,1024]{1,0:T(8,128)(2,1)}, bf16[1024,512]{1,0:T(8,128)(2,1)}) custom-call(bf16[64,2048]{1,0:T(8,128)(2,1)} %tok.1, bf16[2048,256]{1,0:T(8,128)(2,1)} %wq.1, bf16[64,2048]{1,0:T(8,128)(2,1)} %bitcast.4, bf16[64,2048]{1,0:T(8,128)(2,1)} %bitcast.5, bf16[256,2048]{1,0:T(8,128)(2,1)} %wo.1, bf16[1,3,64,128]{3,2,1,0:T(8,128)(2,1)} %pages.1, ...), custom_call_target="tpu_custom_call" | custom-call | tf_op jit(solution)/shard_map/tree_attention/pallas_call | solution.py:627
  43.4 2.2 %convolution_convert_fusion = bf16[64,512]{1,0:T(8,128)(2,1)} fusion(bf16[64,1024]{1,0:T(8,128)(2,1)} %get-tuple-element.7, bf16[1024,512]{1,0:T(8,128)(2,1)} %get-tuple-element.8), kind=kOutput, calls=%fused_computation | convolution fusion | flops 67141632 | bytes 1245184 | tf_op jit(solution)/shard_map/dot_general | solution.py:654

commit v4 on v3

--- a/solution.py
+++ b/solution.py
@@ -227,7 +227,7 @@
         kv_copy(mirror(place, ny)).start()
     forward(0).start()
 
-    for copy in copies[:6]:
+    for copy in copies[:6] + copies[8:12]:
         copy.wait()
     reqs = len_v.shape[1]
     leaves = parent_v.shape[1]
@@ -284,10 +284,8 @@
         )
         return v * cos + swapped * sin
 
-    copies[8].wait()
     wide = tok_v[...].astype(F32)
     normed = (wide * lax.rsqrt(jnp.mean(wide * wide, axis=1, keepdims=True) + EPSILON)).astype(BF16)
-    copies[9].wait()
     queries = jnp.dot(normed, wq_v[...], preferred_element_type=F32)
     for half in range(heads // 2):
         turned = rotated(queries[:, half * LANES : (half + 1) * LANES], cosine, sine)
@@ -296,8 +294,6 @@
         q_copy(place).start()
     for place in range(half_places, ny):
         kv_copy(mirror(place, ny)).start()
-    copies[10].wait()
-    copies[11].wait()
     pack = lax.dot_general(
         normed, wkv_v[...], (((1,), (1,)), ((), ())), preferred_element_type=F32
     )
@@ -385,12 +381,12 @@
         return top, jnp.dot(value, weights, preferred_element_type=F32)
 
     build_queries(0)
+
+    copies[12].wait()
     for place in range(1, ny - 2):
         pass_pages(place)
-
-    copies[12].wait()
-    for pair in range(half_places - 1):
-        build_keys(pair)
+        if place % 2:
+            build_keys(place // 2)
     for place in (0, 1):
         if place < ny - 2:
             forward(place).wait_recv()
@@ -557,6 +553,10 @@
     for step in range(1, nx):
         wo_copy(step).wait_send()
         att_copy(step).wait_send()
+
+
+def product(attended, columns, out):
+    out[...] = jnp.dot(attended[...], columns[...], preferred_element_type=F32).astype(BF16)
 
 
 def local(
@@ -651,7 +651,19 @@
         leaf_parent,
         jnp.asarray(freq, F32),
     )
-    return jnp.dot(attended, columns, preferred_element_type=F32).astype(BF16)
+    depth, steps = attended.shape[1], 2
+    return pl.pallas_call(
+        product,
+        grid=(steps,),
+        out_shape=jax.ShapeDtypeStruct((rows, out_cols), BF16),
+        in_specs=[
+            pl.BlockSpec((rows, depth), lambda at: (0, 0)),
+            pl.BlockSpec((depth, out_cols // steps), lambda at: (0, at)),
+        ],
+        out_specs=pl.BlockSpec((rows, out_cols // steps), lambda at: (0, at)),
+        compiler_params=pltpu.CompilerParams(vmem_limit_bytes=56 << 20),
+        name="output_product",
+    )(attended, columns)
 
 
 def solution(mesh):

time: 46.4 us -> 46.2 us (level)
  matrix products: 2.23 us -> 0 us
  Pallas kernels: 43.4 us -> 45.4 us
    dot_general x1 -> x0, matrix products: 2.23 us -> none  [local(): return jnp.dot(attended, columns, preferred_element_type=F32).astype(BF16)]
    pallas_call x0 -> x1, Pallas kernels: none -> 2.13 us  [local(): pl.pallas_call(product, grid=(steps,), out_shape=jax.ShapeDtypeStruct((ro...]
where the time goes in v4:
time: 46.2 us; the launch traced here: 45.4 us
  Pallas kernels  45.4 us (98%)
    pallas_call x1, Pallas kernels, local(): pl.pallas_call(functools.partial(kernel, (nx, ny, nz, rows, heads)), out_...  43.3 us
    pallas_call x1, Pallas kernels, local(): pl.pallas_call(product, grid=(steps,), out_shape=jax.ShapeDtypeStruct((ro...  2.13 us

profile of v4, /device:TPU:1, one launch (start us, length us, event | category | flops | bytes accessed | tf_op | source)
XLA Modules:
  0.0 45.4 jit_solution(6441743354535332635)
XLA Ops:
  0.0 43.3 %tree_attention.1 = (bf16[64,1024]{1,0:T(8,128)(2,1)}, bf16[1024,512]{1,0:T(8,128)(2,1)}) custom-call(bf16[64,2048]{1,0:T(8,128)(2,1)} %tok.1, bf16[2048,256]{1,0:T(8,128)(2,1)} %wq.1, bf16[64,2048]{1,0:T(8,128)(2,1)} %bitcast.2, bf16[64,2048]{1,0:T(8,128)(2,1)} %bitcast.3, bf16[256,2048]{1,0:T(8,128)(2,1)} %wo.1, bf16[1,3,64,128]{3,2,1,0:T(8,128)(2,1)} %pages.1, ...), custom_call_target="tpu_custom_call" | custom-call | tf_op jit(solution)/shard_map/tree_attention/pallas_call | solution.py:627
  43.3 2.1 %output_product.1 = bf16[64,512]{1,0:T(8,128)(2,1)} custom-call(bf16[64,1024]{1,0:T(8,128)(2,1)} %get-tuple-element.7.attended, bf16[1024,512]{1,0:T(8,128)(2,1)} %get-tuple-element.8.columns), custom_call_target="tpu_custom_call" | custom-call | tf_op jit(solution)/shard_map/output_product/pallas_call | solution.py:655
